TPU v7x, 256 devices: a whole 4x4x8 slice. The times are simulated.
256 devices in a mesh: stream: 32 (over z, y), item: 8 (over x, core).
Axes of the slice: x: 4, y: 4, z: 8, core: 2. Of those that a mesh axis runs over, the one named last changes fastest.
Arguments:
- event_items: int32 [131072], P('stream'), may hold values from 0 to 262143, as said below
- event_sessions: int32 [131072], P('stream'), may hold values from 0 to 8191, never falling along the last dimension, each value on 1 to 64 neighbouring positions
- sketch_bits: int32 [15, 262144], P(None, 'item'), may hold values from 0 to 262143
Outputs:
- sketch: float32 [128, 256], P('stream')
Inputs may be any that keep to these rules, and one draw needn't show every extreme that they name: `event_items`: item 262144 - 1 occurs at least once.
All inputs are finite; a program needn't handle non-finite values.
Results may differ from a plain program's by a relative error of at most 0.0006.
Values may be sent and summed in bfloat16 or wider, within the bound.
No kernel may reach another device: no remote copies, remote signals or barrier semaphores. Data moves between devices by JAX's collectives and lax.ppermute only.
A program may use at most 128 MiB of HBM per device.

v0:
```python
import math
import jax
import jax.numpy as jnp
from jax import lax
from jax.sharding import PartitionSpec as P

SKETCH = 256
WINDOW = 15
ROWS_DEV = 4


def with_halo(shard, sides, width):
    for axis, dim in sides:
        devices, length = (lax.axis_size(axis), shard.shape[dim])
        up = [(i, (i + 1) % devices) for i in range(devices - 1)]
        down = [(j, i) for i, j in up]
        last = lax.slice_in_dim(shard, length - width, length, axis=dim)
        first = lax.slice_in_dim(shard, 0, width, axis=dim)
        before = lax.ppermute(last, axis, up)
        after = lax.ppermute(first, axis, down)
        shard = jnp.concatenate([before, shard, after], axis=dim)
    return shard


def pointwise(count_block, row_margin, col_margin, pair_total):
    log_ratio = (
        jnp.log(jnp.maximum(count_block, 1.0))
        + jnp.log(pair_total)
        - jnp.log(jnp.maximum(row_margin, 1.0))
        - jnp.log(jnp.maximum(col_margin, 1.0))
    )
    return jnp.where(count_block > 0, jnp.maximum(log_ratio, 0.0), 0.0)


def sign_table(bit_block, sketch_width):
    word_count = bit_block.shape[0]
    spread = jnp.repeat(bit_block, 18, axis=0, total_repeat_length=word_count * 18)[:sketch_width]
    bit_shift = (jnp.arange(sketch_width, dtype=jnp.int32) % 18)[:, None]
    return (2 * jnp.bitwise_and(jnp.right_shift(spread, bit_shift), 1) - 1).astype(jnp.float32)


def slab_pairs(ext_items, ext_sessions, row_items):
    extent = ext_items.shape[0]
    own_count = extent - 2 * WINDOW
    own_sessions = ext_sessions[WINDOW : WINDOW + own_count]
    own_items = ext_items[WINDOW : WINDOW + own_count]
    offset = (
        lax.broadcasted_iota(jnp.int32, (own_count, extent), 1)
        - lax.broadcasted_iota(jnp.int32, (own_count, extent), 0)
        - WINDOW
    )
    nearby = (jnp.abs(offset) <= WINDOW) & (offset != 0)
    same_session = own_sessions[:, None] == ext_sessions[None, :]
    banded = (nearby & same_session).astype(jnp.bfloat16)
    row_hot = (
        own_items[None, :] == lax.broadcasted_iota(jnp.int32, (row_items, own_count), 0)
    ).astype(jnp.bfloat16)
    pair_links = lax.dot_general(
        banded, row_hot, (((0,), (1,)), ((), ())), preferred_element_type=jnp.float32
    )
    weights = jnp.sum(banded, axis=0, dtype=jnp.float32)
    return (pair_links, weights)


def tile_block(links_float, ext_items, first_id, col_count):
    local_ids = ext_items - first_id
    in_band = (local_ids >= 0) & (local_ids < col_count)
    return jax.ops.segment_sum(
        jnp.where(in_band[:, None], links_float, 0.0),
        jnp.where(in_band, local_ids, 0),
        num_segments=col_count,
    )


def band_counts(weights, ext_items, first_id, col_count):
    local_ids = ext_items - first_id
    in_band = (local_ids >= 0) & (local_ids < col_count)
    return jax.ops.segment_sum(
        jnp.where(in_band, weights, 0.0), jnp.where(in_band, local_ids, 0), num_segments=col_count
    )


def local(event_items, event_sessions, sketch_bits):
    slab_count = lax.axis_size("stream")
    band_size = sketch_bits.shape[1]
    owned_cols = band_size // slab_count
    row_items = ROWS_DEV * slab_count
    band_start = lax.axis_index("item") * band_size
    own_start = lax.axis_index("stream") * owned_cols
    total_events = event_items.shape[0] * slab_count
    stacked = jnp.stack([event_items, event_sessions + 1])
    extended = with_halo(stacked, (("stream", 1),), WINDOW)
    pair_links, weights = slab_pairs(extended[0], extended[1], row_items)
    band_margin = band_counts(weights, extended[0], band_start, band_size)
    count_tile = lax.psum_scatter(
        tile_block(
            pair_links, extended[0], band_start, owned_cols * lax.axis_size("stream")
        ).astype(jnp.bfloat16),
        "stream",
        scatter_dimension=0,
        tiled=True,
    ).astype(jnp.float32)
    col_margin = lax.psum_scatter(
        band_margin.astype(jnp.bfloat16), "stream", scatter_dimension=0, tiled=True
    ).astype(jnp.float32)
    row_margin, pair_total = lax.psum(
        (jnp.sum(count_tile, axis=0), jnp.sum(col_margin)), ("stream", "item")
    )
    own_bits = lax.dynamic_slice_in_dim(sketch_bits, own_start, owned_cols, 1)
    sign_rows = sign_table(own_bits, SKETCH)
    positive = pointwise(count_tile, row_margin[None, :], col_margin[:, None], pair_total)
    partial_value = lax.dot_general(
        positive,
        sign_rows,
        (((0,), (1,)), ((), ())),
        precision=lax.Precision.HIGHEST,
        preferred_element_type=jnp.float32,
    )
    summed = lax.psum(partial_value, ("stream", "item"))
    own_rows = lax.dynamic_slice_in_dim(summed, lax.axis_index("stream") * ROWS_DEV, ROWS_DEV, 0)
    return own_rows / math.sqrt(total_events)


def solution(mesh):
    placed = (P("stream"), P("stream"), P(None, "item"))
    return jax.shard_map(
        local, mesh=mesh, in_specs=placed, out_specs=P("stream", None), check_vma=False
    )
```

profile of v0, /device:TPU:8, one launch (start us, length us, event | category | flops | bytes accessed | tf_op | source)
XLA Modules:
  0.0 782.7 jit_solution(2511389435921532583)
XLA Ops:
  6.5 0.9 broadcast_add_fusion
  7.4 0.7 fusion.38
  8.2 3.5 collective-permute-start
  11.6 2.4 collective-permute-start.1
  14.0 0.7 pad_add_fusion
  14.8 1.0 iota_compare_fusion.5
  15.8 1.3 collective-permute-done.1
  17.1 0.1 concatenate.7
  17.2 0.1 slice_reduce_fusion
  17.3 0.1 and_reduce_fusion
  17.4 0.1 fusion.35
  17.4 34.8 %convert_reduce_fusion = f32[4126]{0:T(1024)S(1)} fusion(s32[4126]{0:T(1024)S(1)} %slice_reduce_fusion, s32[4096]{0:T(1024)S(1)} %broadcast_add_fusion), kind=kLoop, calls=%fused_computation.3 | loop fusion | flops 185896928 | bytes 49392 | tf_op jit(solution)/shard_map/reduce_sum | solution.py:61
  52.3 28.5 %scatter_custom_fusion.1 = f32[32768]{0:T(1024)S(1)} fusion(s32[4126]{0:T(1024)S(1)} %fusion.35, f32[4126]{0:T(1024)S(1)} %broadcast_select_fusion, f32[]{:T(128)} %constant.122.clone.1), kind=kCustom, calls=%fused_computation.41 | custom fusion | flops 4126 | bytes 131076 | tf_op jit(solution)/shard_map/scatter-add | solution.py:78
  80.8 0.6 convert_element_type.26
  81.4 0.0 all-reduce.7.cloned.1.call-update
  81.4 0.2 reduce-scatter.2.cloned.1.call-start
  81.7 35.3 %fusion.7 = f32[4126,128]{1,0:T(8,128)} fusion(s32[4096]{0:T(1024)S(1)} %broadcast_add_fusion, s32[4126]{0:T(1024)S(1)} %slice_reduce_fusion, pred[4126]{0:T(1024)(128)(4,1)S(1)} %and_reduce_fusion, pred[128,4096]{1,0:T(32,128)(4,1)S(1)} %iota_compare_fusion.5), kind=kOutput, calls=%fused_computation.12 | convolution fusion | flops 4462153728 | bytes 2673814 | tf_op jit(solution)/shard_map/dot_general | solution.py:58
  116.9 32.4 %scatter_custom_fusion = f32[32768,128]{1,0:T(8,128)} fusion(s32[4126]{0:T(1024)S(1)} %fusion.35, f32[4126,128]{1,0:T(8,128)} %fusion.7, f32[]{:T(128)} %constant.122.clone.1), kind=kCustom, calls=%fused_computation.10 | custom fusion | flops 528128 | bytes 16777728 | tf_op jit(solution)/shard_map/scatter-add | solution.py:68
  149.4 9.0 %convert_element_type.22 = bf16[32768,128]{1,0:T(8,128)(2,1)} convert(f32[32768,128]{1,0:T(8,128)} %scatter_custom_fusion) | non-fusion elementwise | flops 4194304 | bytes 25165824 | tf_op jit(solution)/shard_map/convert_element_type | solution.py:98
  158.3 0.0 reduce-scatter.2.cloned.1.call-update
  158.3 0.0 all-reduce.5.cloned.1.call-start
  158.4 0.6 dynamic-slice.6
  159.7 1.8 gather_fusion
  161.5 64.1 %all-reduce.7.cloned.1.call-done = bf16[32768]{0:T(1024)(128)(2,1)} async-done(((bf16[32768]{0:T(1024)(128)(2,1)}), bf16[32768]{0:T(1024)(128)(2,1)}) %all-reduce.7.cloned.1.call-update) | async-done | bytes 65552
  225.6 1.3 convert_reduce_fusion.2
  226.9 229.0 %reduce-scatter.2.cloned.1.call-done = bf16[1024,128]{1,0:T(8,128)(2,1)} async-done(((bf16[32768,128]{1,0:T(8,128)(2,1)}), bf16[1024,128]{1,0:T(8,128)(2,1)}) %reduce-scatter.2.cloned.1.call-update) | async-done | bytes 262160 | tf_op jit(solution)/shard_map/reduce_scatter | solution.py:95
  455.9 1.1 convert_reduce_fusion.1
  457.0 74.3 %all-reduce.1 = (f32[128]{0:T(128)S(1)}, f32[]{:T(128)}) all-reduce(f32[128]{0:T(128)S(1)} %convert_reduce_fusion.1, f32[]{:T(128)} %get-tuple-element.19), channel_id=1, replica_groups=mesh['stream'=32,'item'=8] {'stream','item'}, use_global_device_ids=true, to_apply=%region_8.9 | all-reduce | flops 129 | bytes 1032 | tf_op jit(solution)/shard_map/psum | solution.py:106
  532.0 3.0 fusion.14
  535.0 0.0 all-reduce.5.cloned.1.call-update
  535.0 239.9 %all-reduce.5.cloned.1.call-done = f32[128,256]{1,0:T(8,128)} async-done(((f32[128,256]{1,0:T(8,128)}), f32[128,256]{1,0:T(8,128)}) %all-reduce.5.cloned.1.call-update) | async-done | bytes 131088 | tf_op jit(solution)/shard_map/psum | solution.py:119
  774.9 1.3 dynamic-slice_multiply_fusion
  (13 shorter events, 0.1 us)
Async XLA Ops:
  6.5 153.1 %copy-start = (s32[15,32768]{1,0:T(8,128)S(1)}, s32[15,32768]{1,0:T(8,128)}, u32[]{:S(2)}) copy-start(s32[15,32768]{1,0:T(8,128)} %param.7) | copy-start | bytes 5898244
  6.5 219.0 %all-reduce.7.cloned.1.call-start = ((), (), s32[]{:S(2)}) async-start(), calls=%async_computation.3 | async-start | bytes 131072
  8.2 7.6 collective-permute-start
  11.6 5.5 collective-permute-start.1
  81.4 374.5 %reduce-scatter.2.cloned.1.call-start = ((), (), s32[]{:S(2)}) async-start(), calls=%async_computation.1 | async-start | bytes 8650752 | tf_op jit(solution)/shard_map/reduce_scatter | solution.py:95
  149.4 9.0 %copy-start.2 = (u32[256]{0:T(256)S(1)}, u32[256]{0:T(256)}, u32[]{:S(2)}) copy-start(u32[256]{0:T(256)} %constant.143) | copy-start | bytes 3076
  149.4 10.3 %copy-start.1 = (s32[270]{0:T(512)S(1)}, s32[270]{0:T(512)}, u32[]{:S(2)}) copy-start(s32[270]{0:T(512)} %constant.140) | copy-start | bytes 3244
  158.3 616.5 %all-reduce.5.cloned.1.call-start = ((), (), s32[]{:S(2)}) async-start(), calls=%async_computation.2 | async-start | bytes 262144 | tf_op jit(solution)/shard_map/psum | solution.py:119
Sparse Core Ops, SparseCore 0:
  81.5 143.9 all-reduce.6
  229.6 226.2 reduce-scatter.1
  535.1 239.6 all-reduce.4
where the time goes:
time: 783 us
  waiting for transfers between devices  534 us (68%)
  other arithmetic  113 us (14%)
  blocking collectives  74.3 us (9%)
  matrix products  38.3 us (5%)
  between operations  14.6 us (2%)
    psum x1, waiting for transfers between devices, local(): summed = lax.psum(partial_value, ('stream', 'item'))  240 us
    reduce_scatter x1, waiting for transfers between devices, local(): lax.psum_scatter(tile_block(pair_links, extended[0], band_start, owned_co...  229 us
    psum x1, blocking collectives, local(): lax.psum((jnp.sum(count_tile, axis=0), jnp.sum(col_margin)), ('stream', '...  74.3 us
    unnamed x4, waiting for transfers between devices  64.1 us
    dot_general x1, matrix products, slab_pairs(): lax.dot_general(banded, row_hot, (((0,), (1,)), ((), ())), preferred_elem...  35.3 us
    reduce_sum x1, other arithmetic, slab_pairs(): weights = jnp.sum(banded, axis=0, dtype=jnp.float32)  34.8 us
    scatter-add x1, other arithmetic, tile_block(): jax.ops.segment_sum(jnp.where(in_band[:, None], links_float, 0.0), jnp.wh...  32.4 us
    scatter-add x1, other arithmetic, band_counts(): jax.ops.segment_sum(jnp.where(in_band, weights, 0.0), jnp.where(in_band,...  28.5 us
  transfers between devices with their start and end apart: 5, of which 4 were waited for; matrix products, arithmetic and copies ran while one was open for 10% of the time, Pallas kernels for 0%

commit v1 on v0

--- a/solution.py
+++ b/solution.py
@@ -7,6 +7,11 @@
 SKETCH = 256
 WINDOW = 15
 ROWS_DEV = 4
+
+
+def unite_the_wires(which_axis, field):
+    wide_out = lax.all_gather(field, which_axis)
+    return jnp.sum(wide_out, axis=0)
 
 
 def with_halo(shard, sides, width):
@@ -116,7 +121,7 @@
         precision=lax.Precision.HIGHEST,
         preferred_element_type=jnp.float32,
     )
-    summed = lax.psum(partial_value, ("stream", "item"))
+    summed = unite_the_wires(("stream", "item"), partial_value)
     own_rows = lax.dynamic_slice_in_dim(summed, lax.axis_index("stream") * ROWS_DEV, ROWS_DEV, 0)
     return own_rows / math.sqrt(total_events)
 

time: 783 us -> 706 us (0.902)
  waiting for transfers between devices: 534 us -> 444 us
  other arithmetic: 113 us -> 124 us
    psum x1 -> x0, waiting for transfers between devices: 240 us -> none  [local(): summed = lax.psum(partial_value, ('stream', 'item'))]
    all_gather x0 -> x1, waiting for transfers between devices: none -> 150 us  [unite_the_wires(): wide_out = lax.all_gather(field, which_axis)]
    reduce_sum x0 -> x1, other arithmetic: none -> 12.2 us  [unite_the_wires(): return jnp.sum(wide_out, axis=0)]
  transfers between devices with their start and end apart: 5 -> 5, of which waited for: 4 -> 4; matrix products, arithmetic and copies ran while one was open for 10% -> 12% of each run, Pallas kernels for 0% -> 0%
where the time goes in v1:
time: 706 us; the launch traced here: 704 us
  waiting for transfers between devices  444 us (63%)
  other arithmetic  124 us (18%)
  blocking collectives  74.3 us (11%)
  matrix products  38.2 us (5%)
  between operations  14.6 us (2%)
    reduce_scatter x1, waiting for transfers between devices, local(): lax.psum_scatter(tile_block(pair_links, extended[0], band_start, owned_co...  229 us
    all_gather x1, waiting for transfers between devices, unite_the_wires(): wide_out = lax.all_gather(field, which_axis)  150 us
    psum x1, blocking collectives, local(): lax.psum((jnp.sum(count_tile, axis=0), jnp.sum(col_margin)), ('stream', '...  74.3 us
    unnamed x4, waiting for transfers between devices  63.3 us
    dot_general x1, matrix products, slab_pairs(): lax.dot_general(banded, row_hot, (((0,), (1,)), ((), ())), preferred_elem...  35.3 us
    reduce_sum x1, other arithmetic, slab_pairs(): weights = jnp.sum(banded, axis=0, dtype=jnp.float32)  34.8 us
    scatter-add x1, other arithmetic, tile_block(): jax.ops.segment_sum(jnp.where(in_band[:, None], links_float, 0.0), jnp.wh...  32.4 us
    scatter-add x1, other arithmetic, band_counts(): jax.ops.segment_sum(jnp.where(in_band, weights, 0.0), jnp.where(in_band,...  28.5 us
  transfers between devices with their start and end apart: 5, of which 4 were waited for; matrix products, arithmetic and copies ran while one was open for 12% of the time, Pallas kernels for 0%

profile of v1, /device:TPU:8, one launch (start us, length us, event | category | flops | bytes accessed | tf_op | source)
XLA Modules:
  0.0 704.2 jit_solution(7325858636763912590)
XLA Ops:
  6.5 0.9 broadcast_add_fusion
  7.4 0.7 fusion.38
  8.2 4.1 collective-permute-start.1
  12.2 1.9 collective-permute-start
  14.2 0.7 pad_add_fusion
  14.9 1.0 iota_compare_fusion.5
  16.0 1.7 collective-permute-done
  17.7 0.1 concatenate.7
  17.9 0.1 and_reduce_fusion
  17.9 0.1 fusion.35
  18.0 0.1 slice_reduce_fusion
  18.1 34.8 %convert_reduce_fusion = f32[4126]{0:T(1024)S(1)} fusion(s32[4126]{0:T(1024)S(1)} %slice_reduce_fusion, s32[4096]{0:T(1024)S(1)} %broadcast_add_fusion), kind=kLoop, calls=%fused_computation.3 | loop fusion | flops 185896928 | bytes 49392 | tf_op jit(solution)/shard_map/reduce_sum | solution.py:66
  52.9 28.5 %scatter_custom_fusion.1 = f32[32768]{0:T(1024)S(1)} fusion(s32[4126]{0:T(1024)S(1)} %fusion.35, f32[4126]{0:T(1024)S(1)} %broadcast_select_fusion, f32[]{:T(128)} %constant.122.clone.1), kind=kCustom, calls=%fused_computation.41 | custom fusion | flops 4126 | bytes 131076 | tf_op jit(solution)/shard_map/scatter-add | solution.py:83
  81.4 0.6 convert_element_type.26
  82.0 0.0 all-reduce.4.cloned.1.call-update
  82.0 0.2 reduce-scatter.2.cloned.1.call-start
  82.3 35.3 %fusion.7 = f32[4126,128]{1,0:T(8,128)} fusion(s32[4096]{0:T(1024)S(1)} %broadcast_add_fusion, s32[4126]{0:T(1024)S(1)} %slice_reduce_fusion, pred[4126]{0:T(1024)(128)(4,1)S(1)} %and_reduce_fusion, pred[128,4096]{1,0:T(32,128)(4,1)S(1)} %iota_compare_fusion.5), kind=kOutput, calls=%fused_computation.12 | convolution fusion | flops 4462153728 | bytes 2673814 | tf_op jit(solution)/shard_map/dot_general | solution.py:63
  117.6 32.4 %scatter_custom_fusion = f32[32768,128]{1,0:T(8,128)} fusion(s32[4126]{0:T(1024)S(1)} %fusion.35, f32[4126,128]{1,0:T(8,128)} %fusion.7, f32[]{:T(128)} %constant.122.clone.1), kind=kCustom, calls=%fused_computation.10 | custom fusion | flops 528128 | bytes 16777728 | tf_op jit(solution)/shard_map/scatter-add | solution.py:73
  150.0 9.0 %convert_element_type.22 = bf16[32768,128]{1,0:T(8,128)(2,1)} convert(f32[32768,128]{1,0:T(8,128)} %scatter_custom_fusion) | non-fusion elementwise | flops 4194304 | bytes 25165824 | tf_op jit(solution)/shard_map/convert_element_type | solution.py:103
  159.0 0.0 all-gather.3.cloned.1.call-start
  159.0 0.6 dynamic-slice.6
  160.3 1.8 gather_fusion
  162.2 63.3 %all-reduce.4.cloned.1.call-done = bf16[32768]{0:T(1024)(128)(2,1)} async-done(((bf16[32768]{0:T(1024)(128)(2,1)}), bf16[32768]{0:T(1024)(128)(2,1)}) %all-reduce.4.cloned.1.call-update) | async-done | bytes 65552
  225.4 1.3 convert_reduce_fusion.2
  226.7 229.0 %reduce-scatter.2.cloned.1.call-done = bf16[1024,128]{1,0:T(8,128)(2,1)} async-done(((bf16[32768,128]{1,0:T(8,128)(2,1)}), bf16[1024,128]{1,0:T(8,128)(2,1)}) %reduce-scatter.2.cloned.1.call-update) | async-done | bytes 262160 | tf_op jit(solution)/shard_map/reduce_scatter | solution.py:100
  455.7 1.1 convert_reduce_fusion.1
  456.8 74.3 %all-reduce.1 = (f32[128]{0:T(128)S(1)}, f32[]{:T(128)}) all-reduce(f32[128]{0:T(128)S(1)} %convert_reduce_fusion.1, f32[]{:T(128)} %get-tuple-element.19), channel_id=1, replica_groups=mesh['stream'=32,'item'=8] {'stream','item'}, use_global_device_ids=true, to_apply=%region_8.9 | all-reduce | flops 129 | bytes 1032 | tf_op jit(solution)/shard_map/psum | solution.py:111
  531.9 2.9 fusion.14
  534.8 0.0 all-gather.3.cloned.1.call-update
  534.9 150.0 %all-gather.3.cloned.1.call-done = f32[32768,256]{1,0:T(8,128)} async-done(((f32[128,256]{1,0:T(8,128)}), f32[32768,256]{1,0:T(8,128)}) %all-gather.3.cloned.1.call-update) | async-done | bytes 33554448 | tf_op jit(solution)/shard_map/all_gather | solution.py:13
  684.9 12.2 %reduce_sum.39 = f32[128,256]{1,0:T(8,128)S(1)} reduce(f32[256,128,256]{2,1,0:T(8,128)} %bitcast.7, f32[]{:T(128)} %constant.122.clone.1), dimensions={0}, to_apply=%region_9.10 | reduce | flops 8355840 | bytes 33685508 | tf_op jit(solution)/shard_map/reduce_sum | solution.py:14
  697.1 0.6 dynamic-slice_multiply_fusion
  (14 shorter events, 0.1 us)
Async XLA Ops:
  6.5 153.8 %copy-start = (s32[15,32768]{1,0:T(8,128)S(1)}, s32[15,32768]{1,0:T(8,128)}, u32[]{:S(2)}) copy-start(s32[15,32768]{1,0:T(8,128)} %param.7) | copy-start | bytes 5898244
  6.5 218.9 %all-reduce.4.cloned.1.call-start = ((), (), s32[]{:S(2)}) async-start(), calls=%async_computation.3 | async-start | bytes 131072
  8.2 7.8 %collective-permute-start.1 = (s32[2,15]{1,0:T(2,128)S(1)}, s32[2,15]{1,0:T(2,128)S(1)}, u32[]{:S(2)}, u32[]{:S(2)}) collective-permute-start(s32[2,15]{1,0:T(2,128)S(1)} %get-tuple-element.21), channel_id=1, source_target_pairs={{8,0},{16,8},{24,16},{32,24},{40,32},{48,40},{56,48},{64,56},{72,6... | collective-permute-start | bytes 368 | tf_op jit(solution)/shard_map/ppermute | solution.py:25
  12.2 5.5 collective-permute-start
  82.0 373.7 %reduce-scatter.2.cloned.1.call-start = ((), (), s32[]{:S(2)}) async-start(), calls=%async_computation.1 | async-start | bytes 8650752 | tf_op jit(solution)/shard_map/reduce_scatter | solution.py:100
  150.0 9.1 %copy-start.2 = (u32[256]{0:T(256)S(1)}, u32[256]{0:T(256)}, u32[]{:S(2)}) copy-start(u32[256]{0:T(256)} %constant.143) | copy-start | bytes 3076
  150.0 10.3 %copy-start.1 = (s32[270]{0:T(512)S(1)}, s32[270]{0:T(512)}, u32[]{:S(2)}) copy-start(s32[270]{0:T(512)} %constant.140) | copy-start | bytes 3244
  159.0 525.9 %all-gather.3.cloned.1.call-start = ((), (), s32[]{:S(2)}) async-start(), calls=%async_computation.2 | async-start | bytes 33685504 | tf_op jit(solution)/shard_map/all_gather | solution.py:13
Sparse Core Ops, SparseCore 0:
  82.2 143.2 all-reduce.3
  229.4 226.2 reduce-scatter.1
  535.0 149.8 all-gather.2
